TPU v7x, 128 devices: a whole 4x4x4 slice. The times are simulated.
128 devices in a mesh: req: 8 (over y, core), exp: 16 (over z, x).
Axes of the slice: x: 4, y: 4, z: 4, core: 2. Of those that a mesh axis runs over, the one named last changes fastest.
Arguments:
- hidden: bfloat16 [16384, 2048], P(('req', 'exp')), may hold values from -6 to 6
- lengths: int32 [8, 4], P('req'), may hold values from 1 to 1536, 2048 in all within a row
- attn_gain: float32 [2048], replicated, may hold values from 0.25 to 1.75
- q_gain: float32 [128], replicated, may hold values from 1 to 4.5
- key_norm_gain: float32 [128], replicated, may hold values from 0.1 to 1.9
- w_query: bfloat16 [2048, 4096], P(None, 'exp'), may hold values from -0.125 to 0.125
- key_value_weight: bfloat16 [2048, 1024], replicated, may hold values from -0.125 to 0.125
- w_out: bfloat16 [4096, 2048], P('exp'), may hold values from -0.09375 to 0.09375
- ffn_gain: float32 [2048], replicated, may hold values from 0.25 to 1.75
- w_router: bfloat16 [2048, 128], replicated, may hold values from -0.125 to 0.125
- routes: int32 [16384, 8], P(('req', 'exp')), may hold values from 0 to 127, all different within a row; in each aligned block of 128 rows (0 to 127, 128 to 255, ...) at most 16 rows name the same one
- w_gate: bfloat16 [128, 2048, 768], P(('req', 'exp')), may hold values from -0.125 to 0.125
- w_up: bfloat16 [128, 2048, 768], P(('req', 'exp')), may hold values from -0.125 to 0.125
- w_down: bfloat16 [128, 768, 2048], P(('req', 'exp')), may hold values from -0.21875 to 0.21875
- page_table: int32 [1024], P(('req', 'exp')), may hold values from 0 to 1023, as said below
Outputs:
- layer_out: bfloat16 [16384, 2048], P(('req', 'exp'))
- kv_cache: bfloat16 [1024, 16384], P(('req', 'exp'))
Inputs may be any that keep to these rules, and one draw needn't show every extreme that they name: `routes`: in the rows of one device no expert is named more than 16 times. `page_table`: every page number appears exactly once. The blocks of the device with index (r, x) go to pages held by devices with exp index x, exactly (8) // 8 of them to each req index; the device with flat index i holds pages i * (8) onwards.
All inputs are finite; a program needn't handle non-finite values.
Results may differ from a plain program's by a relative error of at most 0.013.
Values may be sent and summed in bfloat16 or wider, within the bound.
A program may use at most 128 MiB of HBM per device.

v0:
```python
import math
import jax
import jax.numpy as jnp
from jax import lax
from jax.sharding import PartitionSpec as P

EPSILON = 1e-06
THETA_BASE = 1000000.0


def rms_norm(values, scale_gain):
    values = values.astype(jnp.float32)
    factor = lax.rsqrt(jnp.mean(values * values, -1, keepdims=True) + EPSILON)
    return values * factor * scale_gain


def rotate(values, positions):
    half_dim = values.shape[-1] // 2
    freqs = THETA_BASE ** (-jnp.arange(half_dim, dtype=jnp.float32) * 2.0 / values.shape[-1])
    angles = positions.astype(jnp.float32)[:, None] * freqs[None, :]
    cosine = jnp.cos(angles)[:, None, :]
    sine = jnp.sin(angles)[:, None, :]
    first_half = values[..., :half_dim]
    second_half = values[..., half_dim:]
    return jnp.concatenate(
        [first_half * cosine - second_half * sine, second_half * cosine + first_half * sine], -1
    )


def head_prepare(raw, scale_gain, positions, head_dim):
    row_count = raw.shape[0]
    split_heads = raw.reshape(row_count, raw.shape[1] // head_dim, head_dim)
    return (
        rotate(rms_norm(split_heads, scale_gain), positions)
        .reshape(row_count, raw.shape[1])
        .astype(jnp.bfloat16)
    )


def layout(prompt_lengths, row_count):
    ends = jnp.cumsum(prompt_lengths)
    starts = ends - prompt_lengths
    index = jnp.arange(row_count, dtype=jnp.int32)
    inside = (index[:, None] >= starts[None, :]) & (index[:, None] < ends[None, :])
    labels = jnp.arange(prompt_lengths.shape[0], dtype=jnp.int32)
    prompt = jnp.sum(jnp.where(inside, labels[None, :], 0), 1)
    token_position = index - jnp.sum(jnp.where(inside, starts[None, :], 0), 1)
    return (prompt, token_position)


def attend(query, key_rows, values_in, prompt, token_position, head_dim):
    row_count = query.shape[0]
    head_count = query.shape[1] // head_dim
    block_rows = min(512, row_count)
    block_list = row_count // block_rows
    query_blocks = query.reshape(block_list, block_rows, head_count, head_dim)

    def one_block(args):
        query_part, prompt_part, position_part = args
        scores = jnp.einsum(
            "qhd,kd->hqk", query_part, key_rows, preferred_element_type=jnp.float32
        ) / math.sqrt(head_dim)
        allowed = (prompt_part[:, None] == prompt[None, :]) & (
            token_position[None, :] <= position_part[:, None]
        )
        scores = jnp.where(allowed[None], scores, -1e30)
        highest = jnp.max(scores, -1, keepdims=True)
        weights = jnp.exp(scores - highest)
        soft = (weights / jnp.sum(weights, -1, keepdims=True)).astype(jnp.bfloat16)
        mixed = jnp.einsum("hqk,kd->qhd", soft, values_in, preferred_element_type=jnp.float32)
        return mixed.reshape(block_rows, head_count * head_dim).astype(jnp.bfloat16)

    result = lax.map(
        one_block,
        (
            query_blocks,
            prompt.reshape(block_list, block_rows),
            token_position.reshape(block_list, block_rows),
        ),
    )
    return result.reshape(row_count, head_count * head_dim)


def on_device(
    hidden,
    lengths,
    attn_gain,
    q_gain,
    key_norm_gain,
    w_query,
    key_value_weight,
    w_out,
    ffn_gain,
    w_router,
    routes,
    w_gate,
    w_up,
    w_down,
    page_table,
):
    head_dim = q_gain.shape[0]
    kv_heads = key_value_weight.shape[1] // (2 * head_dim)
    local_heads = w_query.shape[1] // head_dim
    query_heads = local_heads * lax.axis_size("exp")
    column = lax.axis_index("exp")
    tokens_here = hidden.shape[0]
    model_width = hidden.shape[1]
    group_rows = tokens_here * lax.axis_size("exp")
    normed = rms_norm(hidden, attn_gain).astype(jnp.bfloat16)
    prompt, token_position = layout(lengths[0], group_rows)
    own_position = lax.dynamic_slice_in_dim(token_position, column * tokens_here, tokens_here)
    key_value = jnp.dot(normed, key_value_weight, preferred_element_type=jnp.float32)
    own_keys = head_prepare(
        key_value[:, : kv_heads * head_dim], key_norm_gain, own_position, head_dim
    )
    own_rows = jnp.concatenate(
        [own_keys, key_value[:, kv_heads * head_dim :].astype(jnp.bfloat16)], 1
    )
    key_value_index = column * local_heads // (query_heads // kv_heads)
    key_cols = key_value_index * head_dim
    value_cols = key_cols + kv_heads * head_dim
    raw = jnp.dot(
        lax.all_gather(normed, "exp", axis=0, tiled=True),
        w_query,
        preferred_element_type=jnp.float32,
    )
    query = head_prepare(raw, q_gain, token_position, head_dim)
    every_row = lax.all_gather(own_rows, "exp", axis=0, tiled=True)
    key_rows = lax.dynamic_slice_in_dim(every_row, key_cols, head_dim, 1)
    value_rows_all = lax.dynamic_slice_in_dim(every_row, value_cols, head_dim, 1)
    mixed = attend(query, key_rows, value_rows_all, prompt, token_position, head_dim)
    projected = lax.psum_scatter(
        jnp.dot(mixed, w_out, preferred_element_type=jnp.float32).astype(jnp.bfloat16),
        "exp",
        scatter_dimension=0,
        tiled=True,
    ).astype(jnp.float32)
    resid = (hidden.astype(jnp.float32) + projected).astype(jnp.bfloat16)
    moe_in = rms_norm(resid, ffn_gain).astype(jnp.bfloat16)
    logits = jnp.dot(moe_in, w_router, preferred_element_type=jnp.float32)
    soft_router = jax.nn.softmax(logits, -1)
    expert_count = w_router.shape[1]
    top_count = routes.shape[1]
    chosen = routes[:, :, None] == jnp.arange(expert_count, dtype=jnp.int32)[None, None, :]
    picked = jnp.sum(jnp.where(chosen, soft_router[:, None, :], 0.0), -1)
    gates = picked / jnp.sum(picked, 1, keepdims=True)
    capacity = 2 * tokens_here * top_count // expert_count
    flat_chosen = chosen.reshape(tokens_here * top_count, expert_count).astype(jnp.int32)
    ranks = jnp.cumsum(flat_chosen, 0) - 1
    slot_ids = jnp.sum(ranks * flat_chosen, 1)
    target = routes.reshape(-1) * capacity + slot_ids
    source_rows = moe_in[jnp.arange(tokens_here * top_count, dtype=jnp.int32) // top_count]
    send_rows = (
        jnp.zeros((expert_count * capacity, model_width), jnp.bfloat16).at[target].set(source_rows)
    )
    direct = send_rows.reshape(expert_count, capacity, model_width)
    batch = lax.all_to_all(direct, ("req", "exp"), split_axis=0, concat_axis=0, tiled=True)
    batch_shape = batch.shape
    rows_flat = batch.reshape(-1, batch_shape[-1])
    gate_part = jnp.dot(rows_flat, w_gate[0], preferred_element_type=jnp.float32)
    up_part = jnp.dot(rows_flat, w_up[0], preferred_element_type=jnp.float32)
    act = (jax.nn.silu(gate_part) * up_part).astype(jnp.bfloat16)
    answer = jnp.dot(act, w_down[0], preferred_element_type=jnp.float32).astype(jnp.bfloat16)
    answered = answer.reshape(batch_shape[:-1] + (w_down.shape[2],))
    returned = lax.all_to_all(answered, ("req", "exp"), split_axis=0, concat_axis=0, tiled=True)
    outcome = returned.reshape(expert_count * capacity, model_width)[target]
    outcome = outcome.reshape(tokens_here, top_count, model_width)
    moe_sum = jnp.sum(outcome.astype(jnp.float32) * gates[:, :, None], 1)
    layer_out = (resid.astype(jnp.float32) + moe_sum).astype(jnp.bfloat16)
    blocks_here = page_table.shape[0]
    page_size = tokens_here // blocks_here
    page_width = page_size * own_rows.shape[1]
    page_blocks = own_rows.reshape(blocks_here, page_width)
    req_count = lax.axis_size("req")
    per_peer = blocks_here // req_count
    owner = page_table // blocks_here // lax.axis_size("exp")
    owner_hit = (owner[:, None] == jnp.arange(req_count, dtype=jnp.int32)[None, :]).astype(
        jnp.int32
    )
    rank_inside = jnp.sum((jnp.cumsum(owner_hit, 0) - 1) * owner_hit, 1)
    send_order = owner * per_peer + rank_inside
    send_pages = jnp.zeros_like(page_blocks).at[send_order].set(page_blocks)
    send_slots = jnp.zeros_like(page_table).at[send_order].set(page_table % blocks_here)
    got_pages, got_slots = (
        lax.all_to_all(
            send_pages.reshape(req_count, per_peer, page_width),
            "req",
            split_axis=0,
            concat_axis=0,
            tiled=True,
        ),
        lax.all_to_all(
            send_slots.reshape(req_count, per_peer), "req", split_axis=0, concat_axis=0, tiled=True
        ),
    )
    kv_cache = (
        jnp.zeros_like(page_blocks)
        .at[got_slots.reshape(-1)]
        .set(got_pages.reshape(blocks_here, page_width))
    )
    return (layer_out, kv_cache)


def solution(mesh):
    in_specs = (
        P(("req", "exp"), None),
        P("req", None),
        P(),
        P(),
        P(),
        P(None, "exp"),
        P(),
        P("exp", None),
        P(),
        P(),
        P(("req", "exp"), None),
        P(("req", "exp"), None, None),
        P(("req", "exp"), None, None),
        P(("req", "exp"), None, None),
        P(("req", "exp")),
    )
    out_specs = (P(("req", "exp"), None), P(("req", "exp"), None))
    return jax.shard_map(
        on_device, mesh=mesh, in_specs=in_specs, out_specs=out_specs, check_vma=False
    )
```

profile of v0, /device:TPU:60, one launch (start us, length us, event | category | flops | bytes accessed | tf_op | source)
XLA Modules:
  0.0 661.6 jit_solution(14308455975298828681)
XLA Ops:
  7.8 1.3 fusion.44
  9.2 2.0 fusion.46
  11.2 3.1 fusion.82
  23.9 6.3 multiply_cosine_fusion
  30.1 43.8 %all-gather.5.cloned.1.call-done = bf16[2048,1024]{1,0:T(8,128)(2,1)} async-done(((bf16[128,1024]{1,0:T(8,128)(2,1)}), bf16[2048,1024]{1,0:T(8,128)(2,1)}) %all-gather.5.cloned.1.call-update) | async-done | bytes 4194320 | tf_op jit(solution)/shard_map/all_gather | solution.py:128
  73.9 2.3 constant_dynamic-slice_fusion.2
  76.2 2.1 copy.88
  78.3 68.8 %all-gather.3.cloned.1.call-done = bf16[2048,2048]{1,0:T(8,128)(2,1)} async-done(((bf16[128,2048]{1,0:T(8,128)(2,1)}), bf16[2048,2048]{1,0:T(8,128)(2,1)}) %all-gather.3.cloned.1.call-update) | async-done | bytes 8388624 | tf_op jit(solution)/shard_map/all_gather | solution.py:123
  147.1 7.4 %multiply_reduce_fusion = (f32[2048,2]{0,1:T(2,128)S(1)}, f32[2048,256]{0,1:T(8,128)}) fusion(bf16[2048,2048]{1,0:T(8,128)(2,1)} %all-gather.3.cloned.1.call-done, bf16[2048,256]{1,0:T(8,128)(2,1)} %param.22), kind=kOutput, calls=%fused_computation.51 | convolution fusion | flops 2148528128 | bytes 11550720 | tf_op jit(solution)/shard_map/dot_general | solution.py:122
  154.5 2.9 copy.84
  157.5 2.1 multiply_multiply_fusion
  160.4 1.6 pad_maximum_fusion
  162.1 69.5 %while.10 = (s32[]{:T(128)}, bf16[4,512,256]{2,1,0:T(8,128)(2,1)}, s32[4,512]{1,0:T(4,128)S(1)}, s32[2048]{0:T(1024)S(1)}, s32[2048]{0:T(1024)S(1)}, /*index=5*/...) while((s32[]{:T(128)}, bf16[4,512,256]{2,1,0:T(8,128)(2,1)}, ...), condition=%wide.region_9.10_spmd, body=%wide.region_6.9_spmd.sunk | while | flops 1089603584 | bytes 21532792 | solution.py:73
  162.1 1.9 compare_and_fusion.2
  164.0 7.9 %fusion.101 = (f32[2,512]{1,0:T(2,128)S(1)}, f32[2,512,2048]{2,1,0:T(8,128)}) fusion(pred[512,2048]{1,0:T(8,128)(4,1)} %compare_and_fusion.2, bf16[2048,128]{1,0:T(8,128)(2,1)} %get-tuple-element.247, bf16[4,512,2,128]{3,1,0,2:T(8,128)(2,1)} %get-tuple-element.246, s32[]{:T(128)S(6)} %copy.117), kind=kOutput, calls=%fused_computation.146.clone.1 | convolution fusion | flops 545261568 | bytes 10227716 | tf_op jit(solution)/shard_map/while/body/eval_jaxpr/sub | solution.py:68
  171.8 5.7 fusion.102
  177.6 1.1 copy.113
  179.4 1.9 compare_and_fusion.2
  181.3 7.9 %fusion.101 = (f32[2,512]{1,0:T(2,128)S(1)}, f32[2,512,2048]{2,1,0:T(8,128)}) fusion(pred[512,2048]{1,0:T(8,128)(4,1)} %compare_and_fusion.2, bf16[2048,128]{1,0:T(8,128)(2,1)} %get-tuple-element.247, bf16[4,512,2,128]{3,1,0,2:T(8,128)(2,1)} %get-tuple-element.246, s32[]{:T(128)S(6)} %copy.117), kind=kOutput, calls=%fused_computation.146.clone.1 | convolution fusion | flops 545261568 | bytes 10227716 | tf_op jit(solution)/shard_map/while/body/eval_jaxpr/sub | solution.py:68
  189.2 5.7 fusion.102
  194.9 1.1 copy.113
  196.7 1.9 compare_and_fusion.2
  198.6 7.9 %fusion.101 = (f32[2,512]{1,0:T(2,128)S(1)}, f32[2,512,2048]{2,1,0:T(8,128)}) fusion(pred[512,2048]{1,0:T(8,128)(4,1)} %compare_and_fusion.2, bf16[2048,128]{1,0:T(8,128)(2,1)} %get-tuple-element.247, bf16[4,512,2,128]{3,1,0,2:T(8,128)(2,1)} %get-tuple-element.246, s32[]{:T(128)S(6)} %copy.117), kind=kOutput, calls=%fused_computation.146.clone.1 | convolution fusion | flops 545261568 | bytes 10227716 | tf_op jit(solution)/shard_map/while/body/eval_jaxpr/sub | solution.py:68
  206.5 5.7 fusion.102
  214.1 1.9 compare_and_fusion.2
  215.9 7.9 %fusion.101 = (f32[2,512]{1,0:T(2,128)S(1)}, f32[2,512,2048]{2,1,0:T(8,128)}) fusion(pred[512,2048]{1,0:T(8,128)(4,1)} %compare_and_fusion.2, bf16[2048,128]{1,0:T(8,128)(2,1)} %get-tuple-element.247, bf16[4,512,2,128]{3,1,0,2:T(8,128)(2,1)} %get-tuple-element.246, s32[]{:T(128)S(6)} %copy.117), kind=kOutput, calls=%fused_computation.146.clone.1 | convolution fusion | flops 545261568 | bytes 10227716 | tf_op jit(solution)/shard_map/while/body/eval_jaxpr/sub | solution.py:68
  223.8 5.7 fusion.102
  231.5 7.1 %convolution_convert_fusion.1 = bf16[2048,2048]{1,0:T(8,128)(2,1)} fusion(bf16[2048,256]{1,0:T(8,128)(2,1)} %bitcast.130, bf16[256,2048]{1,0:T(8,128)(2,1)} %param.24), kind=kOutput, calls=%fused_computation.38 | convolution fusion | flops 2151677952 | bytes 10485760 | tf_op jit(solution)/shard_map/dot_general | solution.py:133
  242.6 80.9 %reduce-scatter.2.cloned.1.call-done = bf16[128,2048]{1,0:T(8,128)(2,1)} async-done(((bf16[2048,2048]{1,0:T(8,128)(2,1)}), bf16[128,2048]{1,0:T(8,128)(2,1)}) %reduce-scatter.2.cloned.1.call-update) | async-done | bytes 524304 | tf_op jit(solution)/shard_map/reduce_scatter | solution.py:132
  323.4 1.5 fusion.48
  324.9 2.2 fusion.50
  327.1 25.1 %scatter_custom_fusion = bf16[2048,2048]{1,0:T(8,128)(2,1)} fusion(s32[1024]{0:T(1024)S(1)} %bitcast.138, bf16[128,2048]{1,0:T(8,128)(2,1)} %fusion.50, s32[1024]{0:T(1024)S(1)} %broadcast_clamp_fusion.1, bf16[]{:T(256)} %constant.128.clone.1), kind=kCustom, calls=%fused_computation.40 | custom fusion | bytes 8389120 | tf_op jit(solution)/shard_map/scatter | solution.py:154
  352.1 9.7 %all-to-all-start = ((bf16[128,16,2048]{2,1,0:T(8,128)(2,1)}), bf16[128,16,2048]{2,1,0:T(8,128)(2,1)}, u32[]{:S(2)}, u32[]{:S(2)}) async-start(bf16[128,16,2048]{2,1,0:T(8,128)(2,1)} %bitcast.126), calls=%async_computation.1 | async-start | bytes 16777216 | tf_op jit(solution)/shard_map/all_to_all | solution.py:157
  364.5 1.4 scatter_custom_fusion.2
  366.5 1.4 reduce.2
  367.9 1.9 reshape.501
  369.7 102.7 %all-to-all-done = bf16[128,16,2048]{2,1,0:T(8,128)(2,1)} async-done(((bf16[128,16,2048]{2,1,0:T(8,128)(2,1)}), bf16[128,16,2048]{2,1,0:T(8,128)(2,1)}, u32[]{:S(2)}, u32[]{:S(2)}) %all-to-all-start) | async-done | bytes 8388640 | tf_op jit(solution)/shard_map/all_to_all | solution.py:157
  472.4 4.5 all-to-all-start.2
  476.9 11.7 %fusion.41 = f32[2048,768]{1,0:T(8,128)} fusion(bf16[2048,2048]{1,0:T(8,128)(2,1)} %bitcast.22, bf16[1,2048,768]{2,1,0:T(8,128)(2,1)} %param.28), kind=kOutput, calls=%fused_computation.45 | convolution fusion | flops 6442450944 | bytes 17825792 | tf_op jit(solution)/shard_map/dot_general | solution.py:160
  488.6 4.8 all-to-all-start.3
  493.4 21.3 %convolution_convert_fusion = bf16[2048,2048]{1,0:T(8,128)(2,1)} fusion(f32[2048,768]{1,0:T(8,128)} %fusion.41, bf16[2048,2048]{1,0:T(8,128)(2,1)} %bitcast.22, bf16[1,768,2048]{2,1,0:T(8,128)(2,1)S(1)} %copy-done, bf16[1,2048,768]{2,1,0:T(8,128)(2,1)} %param.29), kind=kOutput, calls=%fused_computation.37 | convolution fusion | flops 12898533376 | bytes 29360128 | tf_op jit(solution)/shard_map/dot_general | solution.py:163
  514.7 8.5 %all-to-all-start.1 = ((bf16[128,16,2048]{2,1,0:T(8,128)(2,1)}), bf16[128,16,2048]{2,1,0:T(8,128)(2,1)}, u32[]{:S(2)}, u32[]{:S(2)}) async-start(bf16[128,16,2048]{2,1,0:T(8,128)(2,1)} %bitcast.127), calls=%async_computation.2 | async-start | bytes 16777216 | tf_op jit(solution)/shard_map/all_to_all | solution.py:165
  524.4 2.6 scatter_custom_fusion.3
  527.1 1.6 fusion.81
  528.8 2.0 select_reduce_fusion
  530.9 102.8 %all-to-all-done.1 = bf16[128,16,2048]{2,1,0:T(8,128)(2,1)} async-done(((bf16[128,16,2048]{2,1,0:T(8,128)(2,1)}), bf16[128,16,2048]{2,1,0:T(8,128)(2,1)}, u32[]{:S(2)}, u32[]{:S(2)}) %all-to-all-start.1) | async-done | bytes 8388640 | tf_op jit(solution)/shard_map/all_to_all | solution.py:165
  633.7 13.3 %gather_fusion = bf16[1024,2048]{1,0:T(8,128)(2,1)} fusion(bf16[2048,2048]{1,0:T(8,128)(2,1)} %bitcast.27, s32[1024]{0:T(1024)S(1)} %broadcast_clamp_fusion), kind=kCustom, calls=%fused_computation.1 | custom fusion | bytes 8392704 | tf_op jit(solution)/shard_map/gather | solution.py:166
  647.0 6.6 fusion.34
  (104 shorter events, 25.5 us)
Async XLA Ops:
  7.2 486.3 %copy-start = (bf16[1,768,2048]{2,1,0:T(8,128)(2,1)S(1)}, bf16[1,768,2048]{2,1,0:T(8,128)(2,1)}, u32[]{:S(2)}) copy-start(bf16[1,768,2048]{2,1,0:T(8,128)(2,1)} %param.30) | copy-start | bytes 9437188
  7.2 7.8 %copy-start.11 = (s32[1,4]{1,0:T(1,128)S(1)}, s32[1,4]{1,0:T(1,128)}, u32[]{:S(2)}) copy-start(s32[1,4]{1,0:T(1,128)} %param.18) | copy-start | bytes 52
  7.2 66.7 %all-gather.5.cloned.1.call-start = ((), (), s32[]{:S(2)}) async-start(), calls=%async_computation.6 | async-start | bytes 4456448 | tf_op jit(solution)/shard_map/all_gather | solution.py:128
  15.3 0.6 copy-start.7
  21.8 125.3 %all-gather.3.cloned.1.call-start = ((), (), s32[]{:S(2)}) async-start(), calls=%async_computation.5 | async-start | bytes 8912896 | tf_op jit(solution)/shard_map/all_gather | solution.py:123
  22.6 300.9 %reduce-scatter.2.cloned.1.call-start = ((), (), s32[]{:S(2)}) async-start(), calls=%async_computation.7 | async-start | bytes 8912896 | tf_op jit(solution)/shard_map/reduce_scatter | solution.py:132
  154.5 3.0 copy-start.10
  157.5 2.1 copy-start.3
  157.5 2.2 copy-start.4
  238.6 0.7 copy-start.8
  239.3 85.6 %copy-start.9 = (f32[2048]{0:T(1024)S(1)}, f32[2048]{0:T(1024)}, u32[]{:S(2)}) copy-start(f32[2048]{0:T(1024)} %param.25) | copy-start | bytes 24580
  240.1 0.8 copy-start.6
  352.1 9.8 %copy-start.5 = (bf16[128,1024]{1,0:T(8,128)(2,1)S(1)}, bf16[128,1024]{1,0:T(8,128)(2,1)}, u32[]{:S(2)}) copy-start(bf16[128,1024]{1,0:T(8,128)(2,1)} %pad_maximum_fusion.1) | copy-start | bytes 786436
  352.1 10.6 %copy-start.12 = (s32[8]{0:T(128)S(1)}, s32[8]{0:T(128)}, u32[]{:S(2)}) copy-start(s32[8]{0:T(128)} %param.31) | copy-start | bytes 100
  352.1 120.3 %all-to-all-start = ((bf16[128,16,2048]{2,1,0:T(8,128)(2,1)}), bf16[128,16,2048]{2,1,0:T(8,128)(2,1)}, u32[]{:S(2)}, u32[]{:S(2)}) async-start(bf16[128,16,2048]{2,1,0:T(8,128)(2,1)} %bitcast.126), calls=%async_computation.1 | async-start | bytes 16777216 | tf_op jit(solution)/shard_map/all_to_all | solution.py:157
  472.4 16.2 %all-to-all-start.2 = ((s32[8,1,1]{2,1,0:T(1,128)}), s32[8,1,1]{2,1,0:T(1,128)S(1)}, u32[]{:S(2)}, u32[]{:S(2)}) async-start(s32[8,1,1]{2,1,0:T(1,128)} %copy.97), calls=%async_computation.3 | async-start | bytes 8192 | tf_op jit(solution)/shard_map/all_to_all | solution.py:192
  488.6 26.1 %all-to-all-start.3 = ((bf16[8,2,8192]{2,1,0:T(2,128)(2,1)}), bf16[8,2,8192]{2,1,0:T(2,128)(2,1)S(1)}, u32[]{:S(2)}, u32[]{:S(2)}) async-start(bf16[8,2,8192]{2,1,0:T(2,128)(2,1)} %reshape.501), calls=%async_computation.4 | async-start | bytes 524288 | tf_op jit(solution)/shard_map/all_to_all | solution.py:185
  514.7 119.1 %all-to-all-start.1 = ((bf16[128,16,2048]{2,1,0:T(8,128)(2,1)}), bf16[128,16,2048]{2,1,0:T(8,128)(2,1)}, u32[]{:S(2)}, u32[]{:S(2)}) async-start(bf16[128,16,2048]{2,1,0:T(8,128)(2,1)} %bitcast.127), calls=%async_computation.2 | async-start | bytes 16777216 | tf_op jit(solution)/shard_map/all_to_all | solution.py:165
  647.0 6.6 copy-start.1
  647.0 6.6 %copy-start.2 = (bf16[128,2048]{1,0:T(8,128)(2,1)S(1)}, bf16[128,2048]{1,0:T(8,128)(2,1)}, u32[]{:S(2)}) copy-start(bf16[128,2048]{1,0:T(8,128)(2,1)} %reduce-scatter.2.cloned.1.call-done) | copy-start | bytes 1572868
Sparse Core Ops, SparseCore 0:
  21.9 51.9 all-gather.4
  76.6 70.4 all-gather.2
  238.8 84.5 reduce-scatter.1
where the time goes:
time: 666 us; the launch traced here: 662 us
  waiting for transfers between devices  400 us (60%)
  matrix products  106 us (16%)
  local copies, waits for them, and re-layouts  68.1 us (10%)
  other arithmetic  44.4 us (7%)
  starting transfers between devices  28.2 us (4%)
  between operations  14.5 us (2%)
    all_to_all x1, waiting for transfers between devices, on_device(): lax.all_to_all(answered, ('req', 'exp'), split_axis=0, concat_axis=0, til...  103 us
    all_to_all x1, waiting for transfers between devices, on_device(): lax.all_to_all(direct, ('req', 'exp'), split_axis=0, concat_axis=0, tiled...  103 us
    reduce_scatter x1, waiting for transfers between devices, on_device(): lax.psum_scatter(jnp.dot(mixed, w_out, preferred_element_type=jnp.float32...  80.9 us
    all_gather x1, waiting for transfers between devices, on_device(): lax.all_gather(normed, 'exp', axis=0, tiled=True)  68.8 us
    all_gather x1, waiting for transfers between devices, on_device(): every_row = lax.all_gather(own_rows, 'exp', axis=0, tiled=True)  43.8 us
    sub x4, matrix products, one_block(): weights = jnp.exp(scores - highest)  31.5 us
    scatter x1, local copies, waits for them, and re-layouts, on_device(): jnp.zeros((expert_count * capacity, model_width), jnp.bfloat16).at[target]  25.1 us
    dot_general x4, matrix products, one_block(): jnp.einsum('hqk,kd->qhd', soft, values_in, preferred_element_type=jnp.flo...  22.9 us
  transfers between devices with their start and end apart: 7, of which 5 were waited for; matrix products, arithmetic and copies ran while one was open for 9% of the time, Pallas kernels for 0%

commit v1 on v0

--- a/solution.py
+++ b/solution.py
@@ -120,7 +120,9 @@
     key_cols = key_value_index * head_dim
     value_cols = key_cols + kv_heads * head_dim
     raw = jnp.dot(
-        lax.all_gather(normed, "exp", axis=0, tiled=True),
+        jnp.concatenate(
+            lax.all_to_all(jnp.stack([normed] * lax.axis_size("exp")), "exp", 0, 0), axis=0
+        ),
         w_query,
         preferred_element_type=jnp.float32,
     )

time: 666 us -> 699 us (1.050)
  waiting for transfers between devices: 400 us -> 421 us
  local copies, waits for them, and re-layouts: 68.1 us -> 78 us
  starting transfers between devices: 28.2 us -> 36.1 us
    all_gather x1, waiting for transfers between devices: 43.8 us -> 132 us  [on_device(): every_row = lax.all_gather(own_rows, 'exp', axis=0, tiled=True)]
    all_gather x1 -> x0, waiting for transfers between devices: 68.8 us -> none  [on_device(): lax.all_gather(normed, 'exp', axis=0, tiled=True)]
    all_to_all x0 -> x1, starting transfers between devices: none -> 7.97 us  [on_device(): lax.all_to_all(jnp.stack([normed] * lax.axis_size('exp')), 'exp', 0, 0)]
  transfers between devices with their start and end apart: 7 -> 7, of which waited for: 5 -> 4; matrix products, arithmetic and copies ran while one was open for 9% -> 9% of each run, Pallas kernels for 0% -> 0%
where the time goes in v1:
time: 699 us; the launch traced here: 694 us
  waiting for transfers between devices  421 us (60%)
  matrix products  105 us (15%)
  local copies, waits for them, and re-layouts  78 us (11%)
  other arithmetic  38.5 us (6%)
  starting transfers between devices  36.1 us (5%)
  between operations  14.9 us (2%)
    all_gather x1, waiting for transfers between devices, on_device(): every_row = lax.all_gather(own_rows, 'exp', axis=0, tiled=True)  132 us
    all_to_all x1, waiting for transfers between devices, on_device(): lax.all_to_all(answered, ('req', 'exp'), split_axis=0, concat_axis=0, til...  103 us
    all_to_all x1, waiting for transfers between devices, on_device(): lax.all_to_all(direct, ('req', 'exp'), split_axis=0, concat_axis=0, tiled...  103 us
    reduce_scatter x1, waiting for transfers between devices, on_device(): lax.psum_scatter(jnp.dot(mixed, w_out, preferred_element_type=jnp.float32...  83.3 us
    sub x4, matrix products, one_block(): weights = jnp.exp(scores - highest)  31.5 us
    scatter x1, local copies, waits for them, and re-layouts, on_device(): jnp.zeros((expert_count * capacity, model_width), jnp.bfloat16).at[target]  25.1 us
    dot_general x4, matrix products, one_block(): jnp.einsum('hqk,kd->qhd', soft, values_in, preferred_element_type=jnp.flo...  22.9 us
    dot_general x1, matrix products, on_device(): jnp.dot(act, w_down[0], preferred_element_type=jnp.float32)  21.3 us
  transfers between devices with their start and end apart: 7, of which 4 were waited for; matrix products, arithmetic and copies ran while one was open for 9% of the time, Pallas kernels for 0%

profile of v1, /device:TPU:60, one launch (start us, length us, event | category | flops | bytes accessed | tf_op | source)
XLA Modules:
  0.0 694.1 jit_solution(7561252231989651260)
XLA Ops:
  7.8 1.3 fusion.44
  9.1 1.2 fusion.46
  11.1 2.9 fusion.82
  21.5 5.3 stack.2
  26.9 8.0 %all-to-all-start = ((bf16[16,128,2048]{2,1,0:T(8,128)(2,1)}), bf16[16,128,2048]{2,1,0:T(8,128)(2,1)}, u32[]{:S(2)}, u32[]{:S(2)}) async-start(bf16[16,128,2048]{2,1,0:T(8,128)(2,1)} %stack.2), calls=%async_computation | async-start | bytes 16777216 | tf_op jit(solution)/shard_map/all_to_all | solution.py:124
  35.5 2.3 copy.101
  37.8 2.8 multiply_cosine_fusion
  40.6 132.4 %all-gather.2.cloned.1.call-done = bf16[2048,1024]{1,0:T(8,128)(2,1)} async-done(((bf16[128,1024]{1,0:T(8,128)(2,1)}), bf16[2048,1024]{1,0:T(8,128)(2,1)}) %all-gather.2.cloned.1.call-update) | async-done | bytes 4194320 | tf_op jit(solution)/shard_map/all_gather | solution.py:130
  173.0 2.3 constant_dynamic-slice_fusion.2
  175.3 2.0 copy.90
  177.4 6.1 multiply_reduce_fusion
  185.4 2.6 convert_element_type.88
  188.0 2.7 copy.89
  190.7 69.4 %while.10 = (s32[]{:T(128)}, bf16[4,512,256]{2,1,0:T(8,128)(2,1)}, s32[4,512]{1,0:T(4,128)S(1)}, s32[2048]{0:T(1024)S(1)}, s32[2048]{0:T(1024)S(1)}, /*index=5*/...) while((s32[]{:T(128)}, bf16[4,512,256]{2,1,0:T(8,128)(2,1)}, ...), condition=%wide.region_9.10_spmd, body=%wide.region_6.9_spmd.sunk | while | flops 1089603584 | bytes 21532792 | solution.py:73
  190.7 1.9 compare_and_fusion.2
  192.6 7.9 %fusion.101 = (f32[2,512]{1,0:T(2,128)S(1)}, f32[2,512,2048]{2,1,0:T(8,128)}) fusion(pred[512,2048]{1,0:T(8,128)(4,1)} %compare_and_fusion.2, bf16[2048,128]{1,0:T(8,128)(2,1)} %get-tuple-element.247, bf16[4,512,2,128]{3,1,2,0:T(8,128)(2,1)} %get-tuple-element.246, s32[]{:T(128)S(6)} %copy.119), kind=kOutput, calls=%fused_computation.146.clone.1 | convolution fusion | flops 545261568 | bytes 10227716 | tf_op jit(solution)/shard_map/while/body/eval_jaxpr/sub | solution.py:68
  200.5 5.7 fusion.102
  208.0 1.9 compare_and_fusion.2
  209.9 7.9 %fusion.101 = (f32[2,512]{1,0:T(2,128)S(1)}, f32[2,512,2048]{2,1,0:T(8,128)}) fusion(pred[512,2048]{1,0:T(8,128)(4,1)} %compare_and_fusion.2, bf16[2048,128]{1,0:T(8,128)(2,1)} %get-tuple-element.247, bf16[4,512,2,128]{3,1,2,0:T(8,128)(2,1)} %get-tuple-element.246, s32[]{:T(128)S(6)} %copy.119), kind=kOutput, calls=%fused_computation.146.clone.1 | convolution fusion | flops 545261568 | bytes 10227716 | tf_op jit(solution)/shard_map/while/body/eval_jaxpr/sub | solution.py:68
  217.8 5.7 fusion.102
  225.3 1.9 compare_and_fusion.2
  227.2 7.9 %fusion.101 = (f32[2,512]{1,0:T(2,128)S(1)}, f32[2,512,2048]{2,1,0:T(8,128)}) fusion(pred[512,2048]{1,0:T(8,128)(4,1)} %compare_and_fusion.2, bf16[2048,128]{1,0:T(8,128)(2,1)} %get-tuple-element.247, bf16[4,512,2,128]{3,1,2,0:T(8,128)(2,1)} %get-tuple-element.246, s32[]{:T(128)S(6)} %copy.119), kind=kOutput, calls=%fused_computation.146.clone.1 | convolution fusion | flops 545261568 | bytes 10227716 | tf_op jit(solution)/shard_map/while/body/eval_jaxpr/sub | solution.py:68
  235.1 5.7 fusion.102
  242.6 1.9 compare_and_fusion.2
  244.5 7.9 %fusion.101 = (f32[2,512]{1,0:T(2,128)S(1)}, f32[2,512,2048]{2,1,0:T(8,128)}) fusion(pred[512,2048]{1,0:T(8,128)(4,1)} %compare_and_fusion.2, bf16[2048,128]{1,0:T(8,128)(2,1)} %get-tuple-element.247, bf16[4,512,2,128]{3,1,2,0:T(8,128)(2,1)} %get-tuple-element.246, s32[]{:T(128)S(6)} %copy.119), kind=kOutput, calls=%fused_computation.146.clone.1 | convolution fusion | flops 545261568 | bytes 10227716 | tf_op jit(solution)/shard_map/while/body/eval_jaxpr/sub | solution.py:68
  252.4 5.7 fusion.102
  260.1 7.1 %convolution_convert_fusion.1 = bf16[2048,2048]{1,0:T(8,128)(2,1)} fusion(bf16[2048,256]{1,0:T(8,128)(2,1)} %bitcast.131, bf16[256,2048]{1,0:T(8,128)(2,1)} %param.24), kind=kOutput, calls=%fused_computation.38 | convolution fusion | flops 2151677952 | bytes 10485760 | tf_op jit(solution)/shard_map/dot_general | solution.py:135
  271.1 83.3 %reduce-scatter.2.cloned.1.call-done = bf16[128,2048]{1,0:T(8,128)(2,1)} async-done(((bf16[2048,2048]{1,0:T(8,128)(2,1)}), bf16[128,2048]{1,0:T(8,128)(2,1)}) %reduce-scatter.2.cloned.1.call-update) | async-done | bytes 524304 | tf_op jit(solution)/shard_map/reduce_scatter | solution.py:134
  354.5 1.5 fusion.48
  356.0 2.2 fusion.50
  358.2 25.1 %scatter_custom_fusion = bf16[2048,2048]{1,0:T(8,128)(2,1)} fusion(s32[1024]{0:T(1024)S(1)} %bitcast.140, bf16[128,2048]{1,0:T(8,128)(2,1)} %fusion.50, s32[1024]{0:T(1024)S(1)} %broadcast_clamp_fusion.1, bf16[]{:T(256)} %constant.128.clone.1), kind=kCustom, calls=%fused_computation.40 | custom fusion | bytes 8389120 | tf_op jit(solution)/shard_map/scatter | solution.py:156
  383.2 9.7 %all-to-all-start.1 = ((bf16[128,16,2048]{2,1,0:T(8,128)(2,1)}), bf16[128,16,2048]{2,1,0:T(8,128)(2,1)}, u32[]{:S(2)}, u32[]{:S(2)}) async-start(bf16[128,16,2048]{2,1,0:T(8,128)(2,1)} %bitcast.128), calls=%async_computation.2 | async-start | bytes 16777216 | tf_op jit(solution)/shard_map/all_to_all | solution.py:159
  395.6 1.4 scatter_custom_fusion.2
  397.5 1.4 reduce.2
  398.9 1.9 reshape.506
  400.8 102.7 %all-to-all-done.1 = bf16[128,16,2048]{2,1,0:T(8,128)(2,1)} async-done(((bf16[128,16,2048]{2,1,0:T(8,128)(2,1)}), bf16[128,16,2048]{2,1,0:T(8,128)(2,1)}, u32[]{:S(2)}, u32[]{:S(2)}) %all-to-all-start.1) | async-done | bytes 8388640 | tf_op jit(solution)/shard_map/all_to_all | solution.py:159
  503.5 4.5 all-to-all-start.3
  508.0 11.7 %fusion.41 = f32[2048,768]{1,0:T(8,128)} fusion(bf16[2048,2048]{1,0:T(8,128)(2,1)} %bitcast.24, bf16[1,2048,768]{2,1,0:T(8,128)(2,1)} %param.28), kind=kOutput, calls=%fused_computation.45 | convolution fusion | flops 6442450944 | bytes 17825792 | tf_op jit(solution)/shard_map/dot_general | solution.py:162
  519.7 4.8 all-to-all-start.4
  524.5 21.3 %convolution_convert_fusion = bf16[2048,2048]{1,0:T(8,128)(2,1)} fusion(f32[2048,768]{1,0:T(8,128)} %fusion.41, bf16[2048,2048]{1,0:T(8,128)(2,1)} %bitcast.24, bf16[1,768,2048]{2,1,0:T(8,128)(2,1)S(1)} %copy-done, bf16[1,2048,768]{2,1,0:T(8,128)(2,1)} %param.29), kind=kOutput, calls=%fused_computation.37 | convolution fusion | flops 12898533376 | bytes 29360128 | tf_op jit(solution)/shard_map/dot_general | solution.py:165
  545.8 8.5 %all-to-all-start.2 = ((bf16[128,16,2048]{2,1,0:T(8,128)(2,1)}), bf16[128,16,2048]{2,1,0:T(8,128)(2,1)}, u32[]{:S(2)}, u32[]{:S(2)}) async-start(bf16[128,16,2048]{2,1,0:T(8,128)(2,1)} %bitcast.129), calls=%async_computation.3 | async-start | bytes 16777216 | tf_op jit(solution)/shard_map/all_to_all | solution.py:167
  555.5 2.6 scatter_custom_fusion.3
  558.1 1.6 fusion.81
  559.9 2.0 select_reduce_fusion
  562.0 102.8 %all-to-all-done.2 = bf16[128,16,2048]{2,1,0:T(8,128)(2,1)} async-done(((bf16[128,16,2048]{2,1,0:T(8,128)(2,1)}), bf16[128,16,2048]{2,1,0:T(8,128)(2,1)}, u32[]{:S(2)}, u32[]{:S(2)}) %all-to-all-start.2) | async-done | bytes 8388640 | tf_op jit(solution)/shard_map/all_to_all | solution.py:167
  664.8 13.3 %gather_fusion = bf16[1024,2048]{1,0:T(8,128)(2,1)} fusion(bf16[2048,2048]{1,0:T(8,128)(2,1)} %bitcast.29, s32[1024]{0:T(1024)S(1)} %broadcast_clamp_fusion), kind=kCustom, calls=%fused_computation.1 | custom fusion | bytes 8392704 | tf_op jit(solution)/shard_map/gather | solution.py:168
  678.1 6.5 fusion.34
  684.6 2.2 fusion.51
  (110 shorter events, 26.9 us)
Async XLA Ops:
  7.2 517.3 %copy-start = (bf16[1,768,2048]{2,1,0:T(8,128)(2,1)S(1)}, bf16[1,768,2048]{2,1,0:T(8,128)(2,1)}, u32[]{:S(2)}) copy-start(bf16[1,768,2048]{2,1,0:T(8,128)(2,1)} %param.30) | copy-start | bytes 9437188
  7.2 7.6 %copy-start.13 = (s32[1,4]{1,0:T(1,128)S(1)}, s32[1,4]{1,0:T(1,128)}, u32[]{:S(2)}) copy-start(s32[1,4]{1,0:T(1,128)} %param.18) | copy-start | bytes 52
  7.2 165.8 %all-gather.2.cloned.1.call-start = ((), (), s32[]{:S(2)}) async-start(), calls=%async_computation.6 | async-start | bytes 4456448 | tf_op jit(solution)/shard_map/all_gather | solution.py:130
  10.3 0.8 copy-start.1
  15.1 0.6 copy-start.6
  26.8 8.6 %copy-start.7 = (s32[2048]{0:T(1024)S(1)}, s32[2048]{0:T(1024)}, u32[]{:S(2)}) copy-start(s32[2048]{0:T(1024)} %copy-done.6) | copy-start | bytes 24580
  26.9 10.9 %copy-start.8 = (f32[2048]{0:T(1024)S(1)}, f32[2048]{0:T(1024)}, u32[]{:S(2)}) copy-start(f32[2048]{0:T(1024)} %get-tuple-element.147) | copy-start | bytes 24580
  26.9 10.9 %copy-start.11 = (f32[64]{0:T(128)S(1)}, f32[64]{0:T(128)}, u32[]{:S(2)}) copy-start(f32[64]{0:T(128)} %multiply_power_fusion) | copy-start | bytes 772
  26.9 150.5 %all-to-all-start = ((bf16[16,128,2048]{2,1,0:T(8,128)(2,1)}), bf16[16,128,2048]{2,1,0:T(8,128)(2,1)}, u32[]{:S(2)}, u32[]{:S(2)}) async-start(bf16[16,128,2048]{2,1,0:T(8,128)(2,1)} %stack.2), calls=%async_computation | async-start | bytes 16777216 | tf_op jit(solution)/shard_map/all_to_all | solution.py:124
  34.8 319.7 %reduce-scatter.2.cloned.1.call-start = ((), (), s32[]{:S(2)}) async-start(), calls=%async_computation.7 | async-start | bytes 8912896 | tf_op jit(solution)/shard_map/reduce_scatter | solution.py:134
  177.4 6.1 copy-start.12
  177.4 6.5 copy-start.4
  177.4 6.5 copy-start.5
  267.2 0.7 copy-start.9
  267.2 88.7 %copy-start.10 = (f32[2048]{0:T(1024)S(1)}, f32[2048]{0:T(1024)}, u32[]{:S(2)}) copy-start(f32[2048]{0:T(1024)} %param.25) | copy-start | bytes 24580
  268.7 0.8 copy-start.3
  383.2 9.7 %copy-start.2 = (bf16[128,1024]{1,0:T(8,128)(2,1)S(1)}, bf16[128,1024]{1,0:T(8,128)(2,1)}, u32[]{:S(2)}) copy-start(bf16[128,1024]{1,0:T(8,128)(2,1)} %pad_maximum_fusion.1) | copy-start | bytes 786436
  383.2 10.6 %copy-start.14 = (s32[8]{0:T(128)S(1)}, s32[8]{0:T(128)}, u32[]{:S(2)}) copy-start(s32[8]{0:T(128)} %param.31) | copy-start | bytes 100
  383.2 120.3 %all-to-all-start.1 = ((bf16[128,16,2048]{2,1,0:T(8,128)(2,1)}), bf16[128,16,2048]{2,1,0:T(8,128)(2,1)}, u32[]{:S(2)}, u32[]{:S(2)}) async-start(bf16[128,16,2048]{2,1,0:T(8,128)(2,1)} %bitcast.128), calls=%async_computation.2 | async-start | bytes 16777216 | tf_op jit(solution)/shard_map/all_to_all | solution.py:159
  503.5 16.2 %all-to-all-start.3 = ((s32[8,1,1]{2,1,0:T(1,128)}), s32[8,1,1]{2,1,0:T(1,128)S(1)}, u32[]{:S(2)}, u32[]{:S(2)}) async-start(s32[8,1,1]{2,1,0:T(1,128)} %copy.99), calls=%async_computation.4 | async-start | bytes 8192 | tf_op jit(solution)/shard_map/all_to_all | solution.py:194
  519.7 26.1 %all-to-all-start.4 = ((bf16[8,2,8192]{2,1,0:T(2,128)(2,1)}), bf16[8,2,8192]{2,1,0:T(2,128)(2,1)S(1)}, u32[]{:S(2)}, u32[]{:S(2)}) async-start(bf16[8,2,8192]{2,1,0:T(2,128)(2,1)} %reshape.506), calls=%async_computation.5 | async-start | bytes 524288 | tf_op jit(solution)/shard_map/all_to_all | solution.py:187
  545.8 119.0 %all-to-all-start.2 = ((bf16[128,16,2048]{2,1,0:T(8,128)(2,1)}), bf16[128,16,2048]{2,1,0:T(8,128)(2,1)}, u32[]{:S(2)}, u32[]{:S(2)}) async-start(bf16[128,16,2048]{2,1,0:T(8,128)(2,1)} %bitcast.129), calls=%async_computation.3 | async-start | bytes 16777216 | tf_op jit(solution)/shard_map/all_to_all | solution.py:167
Sparse Core Ops, SparseCore 0:
  21.6 151.3 all-gather.1
  267.4 87.0 reduce-scatter.1
